TPU v7x, 32 devices: a whole 2x2x4 slice. The times are simulated.
32 devices in a mesh: groups: 2 (over y), ctx: 4 (over z), dom: 2 (over x), tp: 2 (over core).
Axes of the slice: x: 2, y: 2, z: 4, core: 2. Of those that a mesh axis runs over, the one named last changes fastest.
Arguments:
- queries: bfloat16 [8, 32, 8, 8, 128], P('groups', 'dom', 'tp'), parts along dimension 0, may hold values from -8 to 8
- prompt_cache: bfloat16 [4, 8192, 8, 128], P('groups', 'ctx', 'tp'), parts along dimension 0, may hold values from -8 to 8
- suffix_cache: bfloat16 [4, 32, 16, 8, 128], P('groups', 'dom', 'ctx', 'tp'), parts along dimension 0, may hold values from -8 to 8
- new_kv: bfloat16 [8, 2, 32, 8, 128], P('groups', None, 'dom', 'tp'), parts along dimension 0, may hold values from -8 to 8
- ancestors: int32 [8, 32], P('groups'), parts along dimension 0, may hold values from 0 to 31, as said below
- lengths: int32 [64], P('groups'), parts along dimension 0, may hold values from 1 to 12, as said below
Outputs:
- attended: bfloat16 [8, 32, 8, 8, 128], P('groups', 'dom', 'tp'), parts along dimension 0
There are 2 independent parts, one for each index of `groups`. A program takes and returns all parts, laid end to end along the dimension named above; each array names one. Nothing has to cross between parts.
Inputs may be any that keep to these rules, and one draw needn't show every extreme that they name: `ancestors`: particle p is owned by owner p // 16. In every step, of the 16 offspring of one owner at most 16 have their ancestor among the particles of any one owner, and each owner has exactly 16 from some one owner. `lengths`: the largest length is reached in every draw.
All inputs are finite; a program needn't handle non-finite values.
Results may differ from a plain program's by a relative error of at most 0.005.
Values may be sent and summed in bfloat16 or wider, within the bound.
A program may use at most 128 MiB of HBM per device.

v0:
```python
import math
import jax
import jax.numpy as jnp
from jax import lax
from jax.sharding import PartitionSpec as P


def resample_whole(flat_rows, my_parents, particles):
    one_hot = (my_parents[:, None] == jnp.arange(particles, dtype=jnp.int32)[None, :]).astype(
        jnp.bfloat16
    )
    gathered = jnp.einsum(
        "ji,cir->cjr",
        one_hot,
        lax.all_gather(flat_rows, "dom", axis=1, tiled=True),
        preferred_element_type=jnp.float32,
    )
    return gathered.astype(jnp.bfloat16)


def attend(query_block, prompt_keys, prompt_values, suffix_rows, visible, score_scale):
    prompt_scores = (
        jnp.einsum("pkgh,tkh->kpgt", query_block, prompt_keys, preferred_element_type=jnp.float32)
        * score_scale
    )
    suffix_scores = (
        jnp.einsum(
            "pkgh,pskh->pkgs", query_block, suffix_rows[0], preferred_element_type=jnp.float32
        )
        * score_scale
    )
    suffix_scores = jnp.where(visible[:, None, None, :], suffix_scores, -jnp.inf)
    local_peak = jnp.maximum(
        jnp.transpose(jnp.max(prompt_scores, axis=-1), (1, 0, 2)), jnp.max(suffix_scores, axis=-1)
    )
    peak_score = lax.pmax(local_peak, "ctx")
    prompt_exp = jnp.exp(prompt_scores - jnp.transpose(peak_score, (1, 0, 2))[..., None])
    suffix_exp = jnp.exp(suffix_scores - peak_score[..., None])
    totals = jnp.transpose(jnp.sum(prompt_exp, axis=-1), (1, 0, 2)) + jnp.sum(suffix_exp, axis=-1)
    prompt_weights = prompt_exp.astype(jnp.bfloat16)
    suffix_weights = suffix_exp.astype(jnp.bfloat16)
    numerator = jnp.einsum(
        "kpgt,tkh->pkgh", prompt_weights, prompt_values, preferred_element_type=jnp.float32
    )
    numerator = numerator + jnp.einsum(
        "pkgs,pskh->pkgh", suffix_weights, suffix_rows[1], preferred_element_type=jnp.float32
    )
    total_all, numerator_all = lax.psum((totals, numerator), "ctx")
    return (numerator_all / total_all[..., None]).astype(jnp.bfloat16)


def on_device(queries, prompt_cache, suffix_cache, new_kv, ancestors, lengths):
    my_owner = lax.axis_index("dom")
    my_shard = lax.axis_index("ctx")
    per_owner = queries.shape[1]
    suffix_dev = suffix_cache.shape[2]
    particles = ancestors.shape[1]
    score_scale = 1.0 / math.sqrt(queries.shape[4])
    prompt_keys = prompt_cache[0]
    prompt_values = prompt_cache[1]
    particle_ids = jnp.arange(particles, dtype=jnp.int32)
    positions = my_shard * suffix_dev + jnp.arange(suffix_dev, dtype=jnp.int32)
    suffix_rows = suffix_cache
    lengths_now = lengths
    results = []
    for step_index in range(queries.shape[0]):
        parents = ancestors[step_index]
        my_parents = lax.dynamic_slice_in_dim(parents, my_owner * per_owner, per_owner)
        flat_rows = suffix_rows.reshape(2, per_owner, -1)
        moved_rows = resample_whole(flat_rows, my_parents, particles)
        suffix_rows = moved_rows.reshape(suffix_rows.shape)
        lengths_now = jnp.sum(
            jnp.where(parents[:, None] == particle_ids[None, :], lengths_now[None, :], 0), axis=1
        )
        my_lengths = lax.dynamic_slice_in_dim(lengths_now, my_owner * per_owner, per_owner)
        new_slot = positions[None, :] == my_lengths[:, None]
        suffix_rows = jnp.where(
            new_slot[None, :, :, None, None], new_kv[step_index][:, :, None], suffix_rows
        )
        visible = positions[None, :] <= my_lengths[:, None]
        results.append(
            attend(
                queries[step_index], prompt_keys, prompt_values, suffix_rows, visible, score_scale
            )
        )
        lengths_now = lengths_now + 1
    return jnp.stack(results)


def solution(mesh):
    return jax.shard_map(
        on_device,
        mesh=mesh,
        in_specs=(
            P("groups", "dom", "tp", None, None),
            P("groups", "ctx", "tp", None),
            P("groups", "dom", "ctx", "tp", None),
            P("groups", None, "dom", "tp", None),
            P("groups", None),
            P("groups"),
        ),
        out_specs=P("groups", "dom", "tp", None, None),
        check_vma=False,
    )
```

profile of v0, /device:TPU:0, one launch (start us, length us, event | category | flops | bytes accessed | tf_op | source)
XLA Modules:
  0.0 163.5 jit_solution(15562038349087660170)
XLA Ops:
  8.8 4.1 %fusion.100 = (bf16[1,2048,4,128]{3,2,1,0:T(4,128)(2,1)S(1)}, bf16[1,2048,4,128]{3,2,1,0:T(4,128)(2,1)}) fusion(bf16[2,2048,4,128]{3,2,1,0:T(4,128)(2,1)} %param.7), kind=kLoop, calls=%fused_computation.178 | loop fusion | bytes 8388608 | tf_op jit(solution)/shard_map/slice | solution.py:59
  17.0 7.1 %all_gather.12 = bf16[2,32,2048]{2,1,0:T(8,128)(2,1)S(1)} all-gather(bf16[2,16,2048]{2,1,0:T(8,128)(2,1)S(1)} %reshape.274), channel_id=1, replica_groups=mesh['groups'=2,'ctx'=4,'dom'=2,'tp'=2] {'dom'}, dimensions={1}, use_global_device_ids=true | all-gather | bytes 393216 | tf_op jit(solution)/shard_map/all_gather | solution.py:15
  24.4 5.6 %all_gather.13 = bf16[2,32,2048]{2,1,0:T(8,128)(2,1)S(1)} all-gather(bf16[2,16,2048]{2,1,0:T(8,128)(2,1)S(1)} %get-tuple-element.59), channel_id=1, replica_groups=mesh['groups'=2,'ctx'=4,'dom'=2,'tp'=2] {'dom'}, dimensions={1}, use_global_device_ids=true | all-gather | bytes 393216 | tf_op jit(solution)/shard_map/all_gather | solution.py:15
  30.4 5.6 %all_gather.14 = bf16[2,32,2048]{2,1,0:T(8,128)(2,1)S(1)} all-gather(bf16[2,16,2048]{2,1,0:T(8,128)(2,1)S(1)} %get-tuple-element.61), channel_id=1, replica_groups=mesh['groups'=2,'ctx'=4,'dom'=2,'tp'=2] {'dom'}, dimensions={1}, use_global_device_ids=true | all-gather | bytes 393216 | tf_op jit(solution)/shard_map/all_gather | solution.py:15
  36.3 5.8 %all_gather.15 = bf16[2,32,2048]{2,1,0:T(8,128)(2,1)S(1)} all-gather(bf16[2,16,2048]{2,1,0:T(8,128)(2,1)S(1)} %get-tuple-element.63), channel_id=1, replica_groups=mesh['groups'=2,'ctx'=4,'dom'=2,'tp'=2] {'dom'}, dimensions={1}, use_global_device_ids=true | all-gather | bytes 393216 | tf_op jit(solution)/shard_map/all_gather | solution.py:15
  42.5 4.1 %multiply_reduce_fusion = (f32[4,16,8]{2,1,0:T(8,128)}, f32[4,16,8,2048]{3,2,1,0:T(8,128)}) fusion(bf16[1,2048,4,128]{3,2,1,0:T(4,128)(2,1)S(1)} %get-tuple-element.17, bf16[1,16,4,8,128]{4,3,2,1,0:T(8,128)(2,1)} %get-tuple-element.22), kind=kOutput, calls=%fused_computation.4 | convolution fusion | flops 270532096 | bytes 6424576 | tf_op jit(solution)/shard_map/pkgh,tkh->kpgt/dot_general | solution.py:23
  46.7 3.3 %multiply_reduce_fusion.1 = (f32[4,16,8]{2,1,0:T(8,128)}, f32[4,16,8,2048]{3,2,1,0:T(8,128)}) fusion(bf16[1,2048,4,128]{3,2,1,0:T(4,128)(2,1)S(1)} %get-tuple-element.17, bf16[1,16,4,8,128]{4,3,2,1,0:T(8,128)(2,1)S(1)} %copy-done.10), kind=kOutput, calls=%fused_computation.5 | convolution fusion | flops 270532096 | bytes 6424576 | tf_op jit(solution)/shard_map/pkgh,tkh->kpgt/dot_general | solution.py:23
  50.0 3.3 %multiply_reduce_fusion.2 = (f32[4,16,8]{2,1,0:T(8,128)}, f32[4,16,8,2048]{3,2,1,0:T(8,128)}) fusion(bf16[1,2048,4,128]{3,2,1,0:T(4,128)(2,1)S(1)} %get-tuple-element.17, bf16[1,16,4,8,128]{4,3,2,1,0:T(8,128)(2,1)S(1)} %copy-done.9), kind=kOutput, calls=%fused_computation.6 | convolution fusion | flops 270532096 | bytes 6424576 | tf_op jit(solution)/shard_map/pkgh,tkh->kpgt/dot_general | solution.py:23
  53.5 2.7 %multiply_reduce_fusion.3 = (f32[4,16,8]{2,1,0:T(8,128)S(1)}, f32[4,16,8,2048]{3,2,1,0:T(8,128)}) fusion(bf16[1,2048,4,128]{3,2,1,0:T(4,128)(2,1)S(1)} %get-tuple-element.17, bf16[1,16,4,8,128]{4,3,2,1,0:T(8,128)(2,1)S(1)} %copy-done.8), kind=kOutput, calls=%fused_computation.7 | convolution fusion | flops 270532096 | bytes 6424576 | tf_op jit(solution)/shard_map/pkgh,tkh->kpgt/dot_general | solution.py:23
  56.2 1.1 copy_select_fusion
  57.3 1.6 fusion.102
  58.9 1.4 bitcast_maximum_fusion
  63.2 22.2 %all-reduce.2 = (f32[16,4,8]{2,0,1:T(8,128)S(1)}, f32[16,4,8]{2,0,1:T(8,128)S(1)}, f32[16,4,8]{2,0,1:T(8,128)S(1)}, f32[16,4,8]{2,0,1:T(8,128)S(1)}) all-reduce(f32[16,4,8]{2,0,1:T(8,128)} %bitcast_maximum_fusion, f32[16,4,8]{2,0,1:T(8,128)} %bitcast_maximum_fusion.1, ...), channel_id=1, replica_groups=mesh['groups'=2,'ctx'=4,'dom'=2,'tp'=2] {'ctx'}, use_global_device_ids=true, to_apply=%region_27.28 | all-reduce | flops 2048 | bytes 16384 | tf_op jit(solution)/shard_map/pmax | solution.py:36
  86.6 3.4 %fusion.41 = f32[16,4,8,128]{3,2,0,1:T(8,128)S(1)} fusion(bf16[1,2048,4,128]{3,2,1,0:T(4,128)(2,1)S(1)} %copy-done.6, f32[4,16,8,2048]{3,2,1,0:T(8,128)} %get-tuple-element.58, f32[4,16,8]{2,1,0:T(8,128)S(1)} %bitcast.214), kind=kOutput, calls=%fused_computation.49 | convolution fusion | flops 271581184 | bytes 6555648 | tf_op jit(solution)/shard_map/kpgt,tkh->pkgh/dot_general | solution.py:42
  91.0 1.1 fusion.38
  93.2 1.1 fusion.35
  95.4 1.1 fusion.32
  97.7 3.2 %fusion.6 = f32[4,16,8]{2,1,0:T(8,128)S(1)} fusion(f32[4,16,8,2048]{3,2,1,0:T(8,128)} %get-tuple-element.58, f32[4,16,8]{2,1,0:T(8,128)S(1)} %bitcast.215), kind=kLoop, calls=%fused_computation.14 | loop fusion | flops 3145216 | bytes 4198400 | tf_op jit(solution)/shard_map/reduce_sum | solution.py:39
  104.8 21.4 %all-reduce = (f32[16,4,8]{2,0,1:T(8,128)S(1)}, f32[16,4,8]{2,0,1:T(8,128)S(1)}, f32[16,4,8]{2,0,1:T(8,128)S(1)}, f32[16,4,8]{2,0,1:T(8,128)S(1)}) all-reduce(f32[16,4,8]{2,0,1:T(8,128)S(1)} %bitcast_add_fusion, f32[16,4,8]{2,0,1:T(8,128)S(1)} %bitcast_add_fusion.1, ...), channel_id=1, replica_groups=mesh['groups'=2,'ctx'=4,'dom'=2,'tp'=2] {'ctx'}, use_global_device_ids=true, to_apply=%region_31.32 | all-reduce | flops 2048 | bytes 16384 | tf_op jit(solution)/shard_map/psum | solution.py:48
  126.2 25.2 %all-reduce.5.cloned.1.call-done = (f32[16,4,8,128]{3,2,0,1:T(8,128)}, f32[16,4,8,128]{3,2,0,1:T(8,128)}, f32[16,4,8,128]{3,2,0,1:T(8,128)}, f32[16,4,8,128]{3,2,0,1:T(8,128)}) async-done(((f32[16,4,8,128]{3,2,0,1:T(8,128)}, f32[16,4,8,128]{3,2,0,1:T(8,128)}, f32[16,4,8,128]{3,2,0,1:T(8,128)}, f32[16,4,8,128]{3,2,0,1:T(8,128)}), (f32[16,4,8,128]{3,2,0,1:T(8,128)}, f32[16,4,8,128]{3,2,0,1:T(8,128)}, ...) | async-done | bytes 1048592 | tf_op jit(solution)/shard_map/psum | solution.py:48
  151.3 1.1 fusion.59
  152.4 1.1 fusion.58
  153.5 1.1 fusion.57
  154.6 1.1 fusion.56
  (115 shorter events, 21.1 us)
Async XLA Ops:
  6.5 144.8 %all-reduce.5.cloned.1.call-start = ((), (), s32[]{:S(2)}) async-start(), calls=%async_computation | async-start | bytes 2097152 | tf_op jit(solution)/shard_map/psum | solution.py:48
  8.8 4.1 %copy-start.7 = (bf16[4,16,4,8,128]{4,3,2,1,0:T(8,128)(2,1)S(1)}, bf16[4,16,4,8,128]{4,3,2,1,0:T(8,128)(2,1)}, u32[]{:S(2)}) copy-start(bf16[4,16,4,8,128]{4,3,2,1,0:T(8,128)(2,1)} %param.6) | copy-start | bytes 1572868
  8.8 4.9 %copy-start.18 = (bf16[4,2,16,4,128]{4,3,2,1,0:T(4,128)(2,1)S(1)}, bf16[4,2,16,4,128]{4,3,2,1,0:T(4,128)(2,1)}, u32[]{:S(2)}) copy-start(bf16[4,2,16,4,128]{4,3,2,1,0:T(4,128)(2,1)} %param.9) | copy-start | bytes 393220
  8.8 8.1 %copy-start.19 = (bf16[2,16,4,4,128]{4,3,2,1,0:T(4,128)(2,1)S(1)}, bf16[2,16,4,4,128]{4,3,2,1,0:T(4,128)(2,1)}, u32[]{:S(2)}) copy-start(bf16[2,16,4,4,128]{4,3,2,1,0:T(4,128)(2,1)} %param.8) | copy-start | bytes 393220
  14.4 0.6 copy-start.15
  14.4 2.2 %copy-start.11 = (bf16[2,16,4,128]{3,2,1,0:T(4,128)(2,1)}, bf16[2,16,4,128]{3,2,1,0:T(4,128)(2,1)S(1)}, u32[]{:S(2)}) copy-start(bf16[2,16,4,128]{3,2,1,0:T(4,128)(2,1)S(1)} %get-tuple-element.32) | copy-start | bytes 98308
  14.4 2.2 %copy-start.13 = (bf16[2,16,4,128]{3,2,1,0:T(4,128)(2,1)}, bf16[2,16,4,128]{3,2,1,0:T(4,128)(2,1)S(1)}, u32[]{:S(2)}) copy-start(bf16[2,16,4,128]{3,2,1,0:T(4,128)(2,1)S(1)} %get-tuple-element.33) | copy-start | bytes 98308
  36.3 10.4 %copy-start.10 = (bf16[1,16,4,8,128]{4,3,2,1,0:T(8,128)(2,1)S(1)}, bf16[1,16,4,8,128]{4,3,2,1,0:T(8,128)(2,1)}, u32[]{:S(2)}) copy-start(bf16[1,16,4,8,128]{4,3,2,1,0:T(8,128)(2,1)} %get-tuple-element.20) | copy-start | bytes 393220
  46.7 3.3 %copy-start.9 = (bf16[1,16,4,8,128]{4,3,2,1,0:T(8,128)(2,1)S(1)}, bf16[1,16,4,8,128]{4,3,2,1,0:T(8,128)(2,1)}, u32[]{:S(2)}) copy-start(bf16[1,16,4,8,128]{4,3,2,1,0:T(8,128)(2,1)} %get-tuple-element.21) | copy-start | bytes 393220
  50.0 3.5 %copy-start.8 = (bf16[1,16,4,8,128]{4,3,2,1,0:T(8,128)(2,1)S(1)}, bf16[1,16,4,8,128]{4,3,2,1,0:T(8,128)(2,1)}, u32[]{:S(2)}) copy-start(bf16[1,16,4,8,128]{4,3,2,1,0:T(8,128)(2,1)} %get-tuple-element.19) | copy-start | bytes 393220
  53.4 7.8 %copy-start.17 = (f32[4,16,8]{2,1,0:T(8,128)S(1)}, f32[4,16,8]{2,1,0:T(8,128)}, u32[]{:S(2)}) copy-start(f32[4,16,8]{2,1,0:T(8,128)} %get-tuple-element.67) | copy-start | bytes 6148
  53.5 8.4 %copy-start.12 = (bf16[2,16,4,128]{3,2,1,0:T(4,128)(2,1)S(1)}, bf16[2,16,4,128]{3,2,1,0:T(4,128)(2,1)}, u32[]{:S(2)}) copy-start(bf16[2,16,4,128]{3,2,1,0:T(4,128)(2,1)} %copy-done.11) | copy-start | bytes 98308
  53.5 8.4 %copy-start.14 = (bf16[2,16,4,128]{3,2,1,0:T(4,128)(2,1)S(1)}, bf16[2,16,4,128]{3,2,1,0:T(4,128)(2,1)}, u32[]{:S(2)}) copy-start(bf16[2,16,4,128]{3,2,1,0:T(4,128)(2,1)} %copy-done.13) | copy-start | bytes 98308
  53.5 8.6 %copy-start.21 = (pred[16,4]{1,0:T(8,128)(4,1)S(1)}, pred[16,4]{1,0:T(8,128)(4,1)}, u32[]{:S(2)}) copy-start(pred[16,4]{1,0:T(8,128)(4,1)} %get-tuple-element.52) | copy-start | bytes 196
  53.5 8.8 %copy-start.16 = (f32[4,16,8]{2,1,0:T(8,128)S(1)}, f32[4,16,8]{2,1,0:T(8,128)}, u32[]{:S(2)}) copy-start(f32[4,16,8]{2,1,0:T(8,128)} %get-tuple-element.71) | copy-start | bytes 6148
  53.5 9.5 %copy-start.20 = (pred[16,4]{1,0:T(8,128)(4,1)S(1)}, pred[16,4]{1,0:T(8,128)(4,1)}, u32[]{:S(2)}) copy-start(pred[16,4]{1,0:T(8,128)(4,1)} %get-tuple-element.43) | copy-start | bytes 196
  56.2 30.4 %copy-start.6 = (bf16[1,2048,4,128]{3,2,1,0:T(4,128)(2,1)S(1)}, bf16[1,2048,4,128]{3,2,1,0:T(4,128)(2,1)}, u32[]{:S(2)}) copy-start(bf16[1,2048,4,128]{3,2,1,0:T(4,128)(2,1)} %get-tuple-element.18) | copy-start | bytes 6291460
  86.6 4.4 %copy-start.2 = (f32[4,16,8,2048]{3,2,1,0:T(8,128)S(1)}, f32[4,16,8,2048]{3,2,1,0:T(8,128)}, u32[]{:S(2)}) copy-start(f32[4,16,8,2048]{3,2,1,0:T(8,128)} %get-tuple-element.68) | copy-start | bytes 12582916
  91.0 2.2 %copy-start.4 = (f32[4,16,8,2048]{3,2,1,0:T(8,128)S(1)}, f32[4,16,8,2048]{3,2,1,0:T(8,128)}, u32[]{:S(2)}) copy-start(f32[4,16,8,2048]{3,2,1,0:T(8,128)} %get-tuple-element.72) | copy-start | bytes 12582916
  93.2 2.2 %copy-start = (f32[4,16,8,2048]{3,2,1,0:T(8,128)S(1)}, f32[4,16,8,2048]{3,2,1,0:T(8,128)}, u32[]{:S(2)}) copy-start(f32[4,16,8,2048]{3,2,1,0:T(8,128)} %get-tuple-element.76) | copy-start | bytes 12582916
  97.7 3.5 %copy-start.3 = (f32[4,16,8,2048]{3,2,1,0:T(8,128)S(1)}, f32[4,16,8,2048]{3,2,1,0:T(8,128)}, u32[]{:S(2)}) copy-start(f32[4,16,8,2048]{3,2,1,0:T(8,128)} %get-tuple-element.68) | copy-start | bytes 12582916
  97.7 4.9 %copy-start.5 = (f32[4,16,8,2048]{3,2,1,0:T(8,128)S(1)}, f32[4,16,8,2048]{3,2,1,0:T(8,128)}, u32[]{:S(2)}) copy-start(f32[4,16,8,2048]{3,2,1,0:T(8,128)} %get-tuple-element.72) | copy-start | bytes 12582916
  101.1 2.8 %copy-start.1 = (f32[4,16,8,2048]{3,2,1,0:T(8,128)S(1)}, f32[4,16,8,2048]{3,2,1,0:T(8,128)}, u32[]{:S(2)}) copy-start(f32[4,16,8,2048]{3,2,1,0:T(8,128)} %get-tuple-element.76) | copy-start | bytes 12582916
Sparse Core Ops, SparseCore 0:
  97.8 53.5 all-reduce.4
where the time goes:
time: 164 us
  blocking collectives  67.7 us (41%)
  matrix products  27.9 us (17%)
  waiting for transfers between devices  25.2 us (15%)
  other arithmetic  17.6 us (11%)
  between operations  13.9 us (8%)
  local copies, waits for them, and re-layouts  11.3 us (7%)
    psum x1, waiting for transfers between devices, attend(): total_all, numerator_all = lax.psum((totals, numerator), 'ctx')  25.2 us
    all_gather x4, blocking collectives, resample_whole(): lax.all_gather(flat_rows, 'dom', axis=1, tiled=True)  24.2 us
    pmax x1, blocking collectives, attend(): peak_score = lax.pmax(local_peak, 'ctx')  22.2 us
    psum x1, blocking collectives, attend(): total_all, numerator_all = lax.psum((totals, numerator), 'ctx')  21.4 us
    dot_general x4, matrix products, attend(): jnp.einsum('pkgh,tkh->kpgt', query_block, prompt_keys, preferred_element_...  13.4 us
    dot_general x4, matrix products, attend(): jnp.einsum('kpgt,tkh->pkgh', prompt_weights, prompt_values, preferred_ele...  6.59 us
    reduce_sum x4, other arithmetic, attend(): jnp.sum(prompt_exp, axis=-1)  5.62 us
    another operation x5, other arithmetic, on_device(): return jnp.stack(results)  4.42 us
  transfers between devices with their start and end apart: 1, of which 1 were waited for; matrix products, arithmetic and copies ran while one was open for 3% of the time, Pallas kernels for 0%

commit v1 on v0

--- a/solution.py
+++ b/solution.py
@@ -9,12 +9,27 @@
     one_hot = (my_parents[:, None] == jnp.arange(particles, dtype=jnp.int32)[None, :]).astype(
         jnp.bfloat16
     )
-    gathered = jnp.einsum(
+    size, index = (lax.axis_size("dom"), lax.axis_index("dom"))
+    behind = [(i, (i - 1) % size) for i in range(size)]
+    rows = flat_rows.shape[1]
+    current = flat_rows
+    total = jnp.einsum(
         "ji,cir->cjr",
-        one_hot,
-        lax.all_gather(flat_rows, "dom", axis=1, tiled=True),
+        lax.dynamic_slice_in_dim(one_hot, index * rows, current.shape[1], axis=1),
+        current,
         preferred_element_type=jnp.float32,
     )
+    for turn in range(1, size):
+        current = lax.ppermute(current, "dom", behind)
+        total = total + jnp.einsum(
+            "ji,cir->cjr",
+            lax.dynamic_slice_in_dim(
+                one_hot, (index + turn) % size * rows, current.shape[1], axis=1
+            ),
+            current,
+            preferred_element_type=jnp.float32,
+        )
+    gathered = total
     return gathered.astype(jnp.bfloat16)
 
 

time: 164 us -> 169 us (1.030)
  blocking collectives: 67.7 us -> 44.5 us
  waiting for transfers between devices: 25.2 us -> 35.7 us
  starting transfers between devices: 0.01 us -> 5.28 us
  local copies, waits for them, and re-layouts: 11.3 us -> 15.7 us
  matrix products: 27.9 us -> 32 us
  other arithmetic: 17.6 us -> 21.3 us
    all_gather x4 -> x0, blocking collectives: 24.2 us -> none  [resample_whole(): lax.all_gather(flat_rows, 'dom', axis=1, tiled=True)]
    ppermute x0 -> x4, waiting for transfers between devices: none -> 7.55 us  [resample_whole(): current = lax.ppermute(current, 'dom', behind)]
    ppermute x0 -> x4, starting transfers between devices: none -> 5.28 us  [resample_whole(): current = lax.ppermute(current, 'dom', behind)]
    dot_general x4 -> x8, matrix products: 0.92 us -> 4.55 us  [the longest x4 3.65 us: resample_whole(): jnp.einsum('ji,cir->cjr', lax.dynamic_slice_in_dim(one_hot, (index + turn...]
    psum x1, waiting for transfers between devices: 25.2 us -> 28.1 us  [attend(): total_all, numerator_all = lax.psum((totals, numerator), 'ctx')]
    dot_general x4, matrix products: 6.59 us -> 4.25 us  [attend(): jnp.einsum('kpgt,tkh->pkgh', prompt_weights, prompt_values, preferred_ele...]
    reduce_sum x4, other arithmetic: 5.62 us -> 7.8 us  [attend(): jnp.sum(prompt_exp, axis=-1)]
    broadcast_in_dim x13, local copies, waits for them, and re-layouts: 1.51 us -> 3.31 us  [on_device(): jnp.where(new_slot[None, :, :, None, None], new_kv[step_index][:, :, None...]
  transfers between devices with their start and end apart: 1 -> 5, of which waited for: 1 -> 3; matrix products, arithmetic and copies ran while one was open for 3% -> 22% of each run, Pallas kernels for 0% -> 0%
where the time goes in v1:
time: 169 us; the launch traced here: 168 us
  blocking collectives  44.5 us (26%)
  waiting for transfers between devices  35.7 us (21%)
  matrix products  32 us (19%)
  other arithmetic  21.3 us (13%)
  local copies, waits for them, and re-layouts  15.7 us (9%)
  between operations  13.8 us (8%)
  starting transfers between devices  5.28 us (3%)
    psum x1, waiting for transfers between devices, attend(): total_all, numerator_all = lax.psum((totals, numerator), 'ctx')  28.1 us
    psum x1, blocking collectives, attend(): total_all, numerator_all = lax.psum((totals, numerator), 'ctx')  22.4 us
    pmax x1, blocking collectives, attend(): peak_score = lax.pmax(local_peak, 'ctx')  22.1 us
    dot_general x4, matrix products, attend(): jnp.einsum('pkgh,tkh->kpgt', query_block, prompt_keys, preferred_element_...  15 us
    reduce_sum x4, other arithmetic, attend(): jnp.sum(prompt_exp, axis=-1)  7.8 us
    ppermute x4, waiting for transfers between devices, resample_whole(): current = lax.ppermute(current, 'dom', behind)  7.55 us
    ppermute x4, starting transfers between devices, resample_whole(): current = lax.ppermute(current, 'dom', behind)  5.28 us
    another operation x5, other arithmetic, on_device(): return jnp.stack(results)  4.42 us
  transfers between devices with their start and end apart: 5, of which 3 were waited for; matrix products, arithmetic and copies ran while one was open for 22% of the time, Pallas kernels for 0%

profile of v1, /device:TPU:0, one launch (start us, length us, event | category | flops | bytes accessed | tf_op | source)
XLA Modules:
  0.0 168.3 jit_solution(2464773652439822147)
XLA Ops:
  7.5 3.0 %collective-permute-start = (bf16[2,16,2048]{2,1,0:T(8,128)(2,1)S(1)}, bf16[2,16,2048]{2,1,0:T(8,128)(2,1)}, u32[]{:S(2)}, u32[]{:S(2)}) collective-permute-start(bf16[2,16,2048]{2,1,0:T(8,128)(2,1)S(1)} %reshape.274), channel_id=1, source_target_pairs={{0,2},{2,0},{1,3},{3,1},{4,6},{6,4},{5,7},{7,5},{8,10},{10,8},{9,1... | collective-permute-start | bytes 393224 | tf_op jit(solution)/shard_map/ppermute | solution.py:23
  12.8 4.1 %fusion.120 = (bf16[1,2048,4,128]{3,2,1,0:T(4,128)(2,1)S(1)}, bf16[1,2048,4,128]{3,2,1,0:T(4,128)(2,1)}) fusion(bf16[2,2048,4,128]{3,2,1,0:T(4,128)(2,1)} %param.7), kind=kLoop, calls=%fused_computation.202 | loop fusion | bytes 8388608 | tf_op jit(solution)/shard_map/slice | solution.py:74
  23.9 4.2 %multiply_reduce_fusion = (f32[4,16,8]{2,1,0:T(8,128)}, f32[4,16,8,2048]{3,2,1,0:T(8,128)}) fusion(bf16[1,2048,4,128]{3,2,1,0:T(4,128)(2,1)S(1)} %get-tuple-element.17, bf16[1,16,4,8,128]{4,3,2,1,0:T(8,128)(2,1)} %get-tuple-element.22), kind=kOutput, calls=%fused_computation.4 | convolution fusion | flops 270532096 | bytes 6424576 | tf_op jit(solution)/shard_map/pkgh,tkh->kpgt/dot_general | solution.py:38
  28.1 4.2 %multiply_reduce_fusion.1 = (f32[4,16,8]{2,1,0:T(8,128)}, f32[4,16,8,2048]{3,2,1,0:T(8,128)}) fusion(bf16[1,2048,4,128]{3,2,1,0:T(4,128)(2,1)S(1)} %get-tuple-element.17, bf16[1,16,4,8,128]{4,3,2,1,0:T(8,128)(2,1)} %get-tuple-element.20), kind=kOutput, calls=%fused_computation.5 | convolution fusion | flops 270532096 | bytes 6424576 | tf_op jit(solution)/shard_map/pkgh,tkh->kpgt/dot_general | solution.py:38
  32.3 3.3 %multiply_reduce_fusion.2 = (f32[4,16,8]{2,1,0:T(8,128)}, f32[4,16,8,2048]{3,2,1,0:T(8,128)}) fusion(bf16[1,2048,4,128]{3,2,1,0:T(4,128)(2,1)S(1)} %get-tuple-element.17, bf16[1,16,4,8,128]{4,3,2,1,0:T(8,128)(2,1)S(1)} %copy-done.6), kind=kOutput, calls=%fused_computation.6 | convolution fusion | flops 270532096 | bytes 6424576 | tf_op jit(solution)/shard_map/pkgh,tkh->kpgt/dot_general | solution.py:38
  35.6 3.2 %multiply_reduce_fusion.3 = (f32[4,16,8]{2,1,0:T(8,128)}, f32[4,16,8,2048]{3,2,1,0:T(8,128)}) fusion(bf16[1,2048,4,128]{3,2,1,0:T(4,128)(2,1)S(1)} %get-tuple-element.17, bf16[1,16,4,8,128]{4,3,2,1,0:T(8,128)(2,1)S(1)} %get-tuple-element.19), kind=kOutput, calls=%fused_computation.7 | convolution fusion | flops 270532096 | bytes 6424576 | tf_op jit(solution)/shard_map/pkgh,tkh->kpgt/dot_general | solution.py:38
  39.6 1.1 broadcast_select_fusion.2
  41.1 4.6 %collective-permute-done.1 = bf16[2,16,2048]{2,1,0:T(8,128)(2,1)S(1)} collective-permute-done((bf16[2,16,2048]{2,1,0:T(8,128)(2,1)S(1)}, bf16[2,16,2048]{2,1,0:T(8,128)(2,1)S(1)}, u32[]{:S(2)}, u32[]{:S(2)}) %collective-permute-start.1) | collective-permute-done | bytes 131104 | tf_op jit(solution)/shard_map/ppermute | solution.py:23
  48.4 1.6 fusion.124
  50.0 1.4 bitcast_maximum_fusion.2
  52.9 1.3 broadcast_select_fusion
  54.2 1.8 %collective-permute-start.3 = (bf16[2,16,2048]{2,1,0:T(8,128)(2,1)S(1)}, bf16[2,16,2048]{2,1,0:T(8,128)(2,1)S(1)}, u32[]{:S(2)}, u32[]{:S(2)}) collective-permute-start(bf16[2,16,2048]{2,1,0:T(8,128)(2,1)S(1)} %get-tuple-element.63), channel_id=1, source_target_pairs={{0,2},{2,0},{1,3},{3,1},{4,6},{6,4},{5,7},{7,5},{8,10},{10,8},{9,1... | collective-permute-start | bytes 393224 | tf_op jit(solution)/shard_map/ppermute | solution.py:23
  56.3 2.9 %collective-permute-done.3 = bf16[2,16,2048]{2,1,0:T(8,128)(2,1)S(1)} collective-permute-done((bf16[2,16,2048]{2,1,0:T(8,128)(2,1)S(1)}, bf16[2,16,2048]{2,1,0:T(8,128)(2,1)S(1)}, u32[]{:S(2)}, u32[]{:S(2)}) %collective-permute-start.3) | collective-permute-done | bytes 131104 | tf_op jit(solution)/shard_map/ppermute | solution.py:23
  63.9 22.1 %all-reduce.2 = (f32[16,4,8]{2,0,1:T(8,128)S(1)}, f32[16,4,8]{2,0,1:T(8,128)S(1)}, f32[16,4,8]{2,0,1:T(8,128)S(1)}, f32[16,4,8]{2,0,1:T(8,128)S(1)}) all-reduce(f32[16,4,8]{2,0,1:T(8,128)S(1)} %bitcast_maximum_fusion, f32[16,4,8]{2,0,1:T(8,128)S(1)} %bitcast_maximum_fusion.1, ...), channel_id=1, replica_groups=mesh['groups'=2,'ctx'=4,'dom'=2,'tp'=2] {'ctx'}, use_global_device_ids=true, to_apply=%region_27.28 | all-reduce | flops 2048 | bytes 16384 | tf_op jit(solution)/shard_map/pmax | solution.py:51
  86.1 3.2 %fusion.6 = f32[4,16,8]{2,1,0:T(8,128)S(1)} fusion(f32[4,16,8,2048]{3,2,1,0:T(8,128)} %get-tuple-element.58, f32[4,16,8]{2,1,0:T(8,128)S(1)} %bitcast.230), kind=kLoop, calls=%fused_computation.14 | loop fusion | flops 3145216 | bytes 4198400 | tf_op jit(solution)/shard_map/reduce_sum | solution.py:54
  90.6 1.1 copy-done.2
  93.6 1.3 copy-done.1
  102.6 3.0 %fusion = f32[4,16,8]{2,1,0:T(8,128)S(1)} fusion(f32[4,16,8,2048]{3,2,1,0:T(8,128)} %get-tuple-element.76, f32[4,16,8]{2,1,0:T(8,128)S(1)} %bitcast.225), kind=kLoop, calls=%fused_computation.8 | loop fusion | flops 3145216 | bytes 4198400 | tf_op jit(solution)/shard_map/reduce_sum | solution.py:54
  105.6 22.4 %all-reduce = (f32[16,4,8]{2,0,1:T(8,128)S(1)}, f32[16,4,8]{2,0,1:T(8,128)S(1)}, f32[16,4,8]{2,0,1:T(8,128)S(1)}, f32[16,4,8]{2,0,1:T(8,128)S(1)}) all-reduce(f32[16,4,8]{2,0,1:T(8,128)S(1)} %bitcast_add_fusion, f32[16,4,8]{2,0,1:T(8,128)S(1)} %bitcast_add_fusion.1, ...), channel_id=1, replica_groups=mesh['groups'=2,'ctx'=4,'dom'=2,'tp'=2] {'ctx'}, use_global_device_ids=true, to_apply=%region_31.32 | all-reduce | flops 2048 | bytes 16384 | tf_op jit(solution)/shard_map/psum | solution.py:63
  128.0 28.1 %all-reduce.5.cloned.1.call-done = (f32[16,4,8,128]{3,2,0,1:T(8,128)}, f32[16,4,8,128]{3,2,0,1:T(8,128)}, f32[16,4,8,128]{3,2,0,1:T(8,128)}, f32[16,4,8,128]{3,2,0,1:T(8,128)}) async-done(((f32[16,4,8,128]{3,2,0,1:T(8,128)}, f32[16,4,8,128]{3,2,0,1:T(8,128)}, f32[16,4,8,128]{3,2,0,1:T(8,128)}, f32[16,4,8,128]{3,2,0,1:T(8,128)}), (f32[16,4,8,128]{3,2,0,1:T(8,128)}, f32[16,4,8,128]{3,2,0,1:T(8,128)}, ...) | async-done | bytes 1048592 | tf_op jit(solution)/shard_map/psum | solution.py:63
  156.1 1.1 fusion.63
  157.2 1.1 fusion.62
  158.3 1.1 fusion.61
  159.4 1.1 fusion.60
  (123 shorter events, 32.1 us)
Async XLA Ops:
  6.5 149.5 %all-reduce.5.cloned.1.call-start = ((), (), s32[]{:S(2)}) async-start(), calls=%async_computation | async-start | bytes 2097152 | tf_op jit(solution)/shard_map/psum | solution.py:63
  7.5 32.0 %collective-permute-start = (bf16[2,16,2048]{2,1,0:T(8,128)(2,1)S(1)}, bf16[2,16,2048]{2,1,0:T(8,128)(2,1)}, u32[]{:S(2)}, u32[]{:S(2)}) collective-permute-start(bf16[2,16,2048]{2,1,0:T(8,128)(2,1)S(1)} %reshape.274), channel_id=1, source_target_pairs={{0,2},{2,0},{1,3},{3,1},{4,6},{6,4},{5,7},{7,5},{8,10},{10,8},{9,1... | collective-permute-start | bytes 393224 | tf_op jit(solution)/shard_map/ppermute | solution.py:23
  12.8 4.1 %copy-start.5 = (bf16[4,16,4,8,128]{4,3,2,1,0:T(8,128)(2,1)S(1)}, bf16[4,16,4,8,128]{4,3,2,1,0:T(8,128)(2,1)}, u32[]{:S(2)}) copy-start(bf16[4,16,4,8,128]{4,3,2,1,0:T(8,128)(2,1)} %param.6) | copy-start | bytes 1572868
  12.8 4.9 %copy-start.13 = (bf16[4,2,16,4,128]{4,3,2,1,0:T(4,128)(2,1)S(1)}, bf16[4,2,16,4,128]{4,3,2,1,0:T(4,128)(2,1)}, u32[]{:S(2)}) copy-start(bf16[4,2,16,4,128]{4,3,2,1,0:T(4,128)(2,1)} %param.9) | copy-start | bytes 393220
  18.3 3.4 %copy-start.10 = (bf16[2,16,4,128]{3,2,1,0:T(4,128)(2,1)}, bf16[2,16,4,128]{3,2,1,0:T(4,128)(2,1)S(1)}, u32[]{:S(2)}) copy-start(bf16[2,16,4,128]{3,2,1,0:T(4,128)(2,1)S(1)} %get-tuple-element.32) | copy-start | bytes 98308
  18.3 4.4 %copy-start.11 = (bf16[2,16,4,128]{3,2,1,0:T(4,128)(2,1)}, bf16[2,16,4,128]{3,2,1,0:T(4,128)(2,1)S(1)}, u32[]{:S(2)}) copy-start(bf16[2,16,4,128]{3,2,1,0:T(4,128)(2,1)S(1)} %get-tuple-element.33) | copy-start | bytes 98308
  20.0 1.7 %copy-start.16 = (pred[16,4]{1,0:T(8,128)(4,1)}, pred[16,4]{1,0:T(8,128)(4,1)S(1)}, u32[]{:S(2)}) copy-start(pred[16,4]{1,0:T(8,128)(4,1)S(1)} %get-tuple-element.53) | copy-start | bytes 196
  20.0 1.7 %copy-start.18 = (pred[16,4]{1,0:T(8,128)(4,1)}, pred[16,4]{1,0:T(8,128)(4,1)S(1)}, u32[]{:S(2)}) copy-start(pred[16,4]{1,0:T(8,128)(4,1)S(1)} %get-tuple-element.51) | copy-start | bytes 196
  20.0 2.7 %copy-start.17 = (pred[16,4]{1,0:T(8,128)(4,1)}, pred[16,4]{1,0:T(8,128)(4,1)S(1)}, u32[]{:S(2)}) copy-start(pred[16,4]{1,0:T(8,128)(4,1)S(1)} %get-tuple-element.44) | copy-start | bytes 196
  28.1 4.2 %copy-start.6 = (bf16[1,16,4,8,128]{4,3,2,1,0:T(8,128)(2,1)S(1)}, bf16[1,16,4,8,128]{4,3,2,1,0:T(8,128)(2,1)}, u32[]{:S(2)}) copy-start(bf16[1,16,4,8,128]{4,3,2,1,0:T(8,128)(2,1)} %get-tuple-element.21) | copy-start | bytes 393220
  38.9 12.5 %copy-start.19 = (pred[16,4]{1,0:T(8,128)(4,1)S(1)}, pred[16,4]{1,0:T(8,128)(4,1)}, u32[]{:S(2)}) copy-start(pred[16,4]{1,0:T(8,128)(4,1)} %get-tuple-element.43) | copy-start | bytes 196
  38.9 13.4 %copy-start.12 = (f32[4,16,8]{2,1,0:T(8,128)S(1)}, f32[4,16,8]{2,1,0:T(8,128)}, u32[]{:S(2)}) copy-start(f32[4,16,8]{2,1,0:T(8,128)} %get-tuple-element.75) | copy-start | bytes 6148
  40.7 5.0 %collective-permute-start.1 = (bf16[2,16,2048]{2,1,0:T(8,128)(2,1)S(1)}, bf16[2,16,2048]{2,1,0:T(8,128)(2,1)S(1)}, u32[]{:S(2)}, u32[]{:S(2)}) collective-permute-start(bf16[2,16,2048]{2,1,0:T(8,128)(2,1)S(1)} %get-tuple-element.59), channel_id=1, source_target_pairs={{0,2},{2,0},{1,3},{3,1},{4,6},{6,4},{5,7},{7,5},{8,10},{10,8},{9,1... | collective-permute-start | bytes 393224 | tf_op jit(solution)/shard_map/ppermute | solution.py:23
  46.7 6.1 %collective-permute-start.2 = (bf16[2,16,2048]{2,1,0:T(8,128)(2,1)S(1)}, bf16[2,16,2048]{2,1,0:T(8,128)(2,1)}, u32[]{:S(2)}, u32[]{:S(2)}) collective-permute-start(bf16[2,16,2048]{2,1,0:T(8,128)(2,1)S(1)} %get-tuple-element.61), channel_id=1, source_target_pairs={{0,2},{2,0},{1,3},{3,1},{4,6},{6,4},{5,7},{7,5},{8,10},{10,8},{9,1... | collective-permute-start | bytes 393224 | tf_op jit(solution)/shard_map/ppermute | solution.py:23
  48.4 3.9 %copy-start.7 = (bf16[2,16,4,4,128]{4,2,3,1,0:T(4,128)(2,1)}, bf16[2,16,4,4,128]{4,2,3,1,0:T(4,128)(2,1)S(1)}, u32[]{:S(2)}) copy-start(bf16[2,16,4,4,128]{4,2,3,1,0:T(4,128)(2,1)S(1)} %get-tuple-element.81) | copy-start | bytes 393220
  52.9 36.4 %copy-start.4 = (bf16[1,2048,4,128]{3,2,1,0:T(4,128)(2,1)S(1)}, bf16[1,2048,4,128]{3,2,1,0:T(4,128)(2,1)}, u32[]{:S(2)}) copy-start(bf16[1,2048,4,128]{3,2,1,0:T(4,128)(2,1)} %get-tuple-element.18) | copy-start | bytes 6291460
  54.2 5.0 %collective-permute-start.3 = (bf16[2,16,2048]{2,1,0:T(8,128)(2,1)S(1)}, bf16[2,16,2048]{2,1,0:T(8,128)(2,1)S(1)}, u32[]{:S(2)}, u32[]{:S(2)}) collective-permute-start(bf16[2,16,2048]{2,1,0:T(8,128)(2,1)S(1)} %get-tuple-element.63), channel_id=1, source_target_pairs={{0,2},{2,0},{1,3},{3,1},{4,6},{6,4},{5,7},{7,5},{8,10},{10,8},{9,1... | collective-permute-start | bytes 393224 | tf_op jit(solution)/shard_map/ppermute | solution.py:23
  86.1 3.5 %copy-start.3 = (f32[4,16,8,2048]{3,2,1,0:T(8,128)S(1)}, f32[4,16,8,2048]{3,2,1,0:T(8,128)}, u32[]{:S(2)}) copy-start(f32[4,16,8,2048]{3,2,1,0:T(8,128)} %get-tuple-element.58) | copy-start | bytes 12582916
  89.5 2.2 %copy-start.2 = (f32[4,16,8,2048]{3,2,1,0:T(8,128)S(1)}, f32[4,16,8,2048]{3,2,1,0:T(8,128)}, u32[]{:S(2)}) copy-start(f32[4,16,8,2048]{3,2,1,0:T(8,128)} %get-tuple-element.68) | copy-start | bytes 12582916
  92.8 2.2 %copy-start.1 = (f32[4,16,8,2048]{3,2,1,0:T(8,128)S(1)}, f32[4,16,8,2048]{3,2,1,0:T(8,128)}, u32[]{:S(2)}) copy-start(f32[4,16,8,2048]{3,2,1,0:T(8,128)} %get-tuple-element.72) | copy-start | bytes 12582916
  96.0 3.1 %copy-start.15 = (f32[16,4,8,4]{2,3,1,0:T(4,128)S(1)}, f32[16,4,8,4]{2,3,1,0:T(4,128)}, u32[]{:S(2)}) copy-start(f32[16,4,8,4]{2,3,1,0:T(4,128)} %get-tuple-element.74) | copy-start | bytes 24580
  96.0 3.3 %copy-start.8 = (bf16[2,16,4,4,128]{4,2,3,1,0:T(4,128)(2,1)S(1)}, bf16[2,16,4,4,128]{4,2,3,1,0:T(4,128)(2,1)}, u32[]{:S(2)}) copy-start(bf16[2,16,4,4,128]{4,2,3,1,0:T(4,128)(2,1)} %copy-done.7) | copy-start | bytes 393220
  96.0 4.2 %copy-start = (f32[4,16,8,2048]{3,2,1,0:T(8,128)S(1)}, f32[4,16,8,2048]{3,2,1,0:T(8,128)}, u32[]{:S(2)}) copy-start(f32[4,16,8,2048]{3,2,1,0:T(8,128)} %get-tuple-element.76) | copy-start | bytes 12582916
  100.3 1.1 copy-start.14
  (1 other events, 0.6 us)
Sparse Core Ops, SparseCore 0:
  102.6 53.3 all-reduce.4
